TPU v7x, 128 devices: a whole 4x4x4 slice. The times are simulated.
128 devices in a mesh: req: 32 (over z, x, core), tp: 4 (over y).
Axes of the slice: x: 4, y: 4, z: 4, core: 2. Of those that a mesh axis runs over, the one named last changes fastest.
Arguments:
- tokens: bfloat16 [16384, 2560], P('req'), may hold values from -6 to 6
- lengths: int32 [32], P('req'), may hold values from 1 to 512, as said below
- page_slot: int32 [128], replicated, may hold values from 0 to 127, as said below
- trainer_layout: int32 [128], replicated, may hold values from 0 to 127, each once
- trainer_qkv: float32 [2560, 3840], P(('req', 'tp'))
- trainer_gateup: float32 [2560, 13824], P(('req', 'tp')), may hold values from -0.125 to 0.125
- attn_gain: float32 [2560], replicated, may hold values from 0.1 to 1.9
- ffn_gain: float32 [2560], replicated, may hold values from 0.1 to 1.9
- out_proj: bfloat16 [2560, 2560], P('tp'), may hold values from -0.125 to 0.125
- down_proj: bfloat16 [6912, 2560], P('tp'), may hold values from -0.078125 to 0.078125
Outputs:
- layer_out: bfloat16 [16384, 2560], P(('req', 'tp'))
- kv_cache: bfloat16 [128, 128, 1280], P('req', None, 'tp')
Inputs may be any that keep to these rules, and one draw needn't show every extreme that they name: `lengths`: heavy-tailed; some request has exactly 512. `page_slot`: a permutation; pool slot s belongs to request device s // 4; the 4 pages of one request belong to 4 different devices. `trainer_layout`: a permutation; shard s is the trainer shard on the device with index s over req and tp together.
All inputs are finite; a program needn't handle non-finite values.
Results may differ from a plain program's by a relative error of at most 0.0065.
The roundings to bfloat16 on the way count: a program that leaves them out, or rounds other values in their place, can miss the bound.
Values may be sent and summed in bfloat16 or wider, within the bound.
A program may use at most 192 MiB of HBM per device.

v0:
```python
import jax
import jax.numpy as jnp
from jax import lax
from jax.sharding import PartitionSpec as P

HD = 80
PAGE = 128
eps_norm = 1e-05
theta_base = 10000.0


def normed(values, gain):
    scale = lax.rsqrt(jnp.mean(values * values, axis=-1, keepdims=True) + eps_norm)
    return (values * scale * gain).astype(jnp.bfloat16)


def rotary(field, head_dim):
    half = head_dim // 2
    count = field.shape[0]
    freq = theta_base ** (-jnp.arange(half, dtype=jnp.float32) * 2.0 / head_dim)
    angles = jnp.arange(count, dtype=jnp.float32)[:, None] * freq[None, :]
    cosine = jnp.cos(angles)[:, None, :]
    sine = jnp.sin(angles)[:, None, :]
    first = field[..., :half]
    second = field[..., half:]
    return jnp.concatenate(
        [first * cosine - second * sine, second * cosine + first * sine], axis=-1
    )


def body(
    tokens,
    lengths,
    page_slot,
    trainer_layout,
    trainer_qkv,
    trainer_gateup,
    attn_gain,
    ffn_gain,
    out_proj,
    down_proj,
):
    n_tp = lax.axis_size("tp")
    n_req = lax.axis_size("req")
    devices = n_tp * n_req
    rows_each = trainer_qkv.shape[0]
    seq_len = tokens.shape[0]
    model_dim = tokens.shape[1]
    head_dim = HD
    local_heads = out_proj.shape[0] // head_dim
    group_cols = trainer_qkv.shape[1] // n_tp
    local_kv = (group_cols // head_dim - local_heads) // 2
    group = local_heads // local_kv
    q_cols = local_heads * head_dim
    k_cols = local_kv * head_dim
    ff_local = down_proj.shape[0]
    qkv_half, gu_half = (
        lax.all_to_all(
            trainer_qkv.astype(jnp.bfloat16), "tp", split_axis=1, concat_axis=0, tiled=True
        ),
        lax.all_to_all(
            trainer_gateup.astype(jnp.bfloat16), "tp", split_axis=1, concat_axis=0, tiled=True
        ),
    )
    x_f = tokens.astype(jnp.float32)
    x_norm = normed(x_f, attn_gain)
    inverse = (
        jnp.zeros((devices,), jnp.int32)
        .at[trainer_layout]
        .set(jnp.arange(devices, dtype=jnp.int32))
    )
    qkv_all, gu_all = (
        lax.all_gather(qkv_half, "req", axis=0, tiled=True),
        lax.all_gather(gu_half, "req", axis=0, tiled=True),
    )
    qkv_weight = qkv_all.reshape(devices, rows_each, qkv_all.shape[1])[inverse].reshape(
        model_dim, qkv_all.shape[1]
    )
    gu_weight = gu_all.reshape(devices, rows_each, gu_all.shape[1])[inverse].reshape(
        model_dim, gu_all.shape[1]
    )
    joined = jnp.dot(x_norm, qkv_weight, preferred_element_type=jnp.float32)
    query = rotary(joined[:, :q_cols].reshape(seq_len, local_heads, head_dim), head_dim)
    keys = rotary(
        joined[:, q_cols : q_cols + k_cols].reshape(seq_len, local_kv, head_dim), head_dim
    )
    query16 = query.astype(jnp.bfloat16).reshape(seq_len, local_kv, group, head_dim)
    keys16 = keys.astype(jnp.bfloat16)
    values16 = (
        joined[:, q_cols + k_cols :].reshape(seq_len, local_kv, head_dim).astype(jnp.bfloat16)
    )
    scores = jnp.einsum(
        "qkgd,skd->kgqs", query16, keys16, preferred_element_type=jnp.float32
    ) * head_dim ** (-0.5)
    slots = jnp.arange(seq_len, dtype=jnp.int32)
    length = lengths[0]
    allowed = (slots[None, :] <= slots[:, None]) & (slots[None, :] < length)
    scores = jnp.where(allowed[None, None], scores, -1e30)
    probs = jax.nn.softmax(scores, axis=-1).astype(jnp.bfloat16)
    context = jnp.einsum(
        "kgqs,skd->qkgd", probs, values16, preferred_element_type=jnp.float32
    ).astype(jnp.bfloat16)
    partial_out = jnp.dot(
        context.reshape(seq_len, q_cols), out_proj, preferred_element_type=jnp.float32
    )
    share = seq_len // n_tp
    tp_index = lax.axis_index("tp")
    mixed = lax.psum(partial_out, "tp")
    resid = x_f + mixed
    h_norm = normed(resid, ffn_gain)
    resid_share = lax.dynamic_slice_in_dim(resid, tp_index * share, share, 0)
    projected = jnp.dot(h_norm, gu_weight, preferred_element_type=jnp.float32)
    hidden = (jax.nn.silu(projected[:, :ff_local]) * projected[:, ff_local:]).astype(jnp.bfloat16)
    down = jnp.dot(hidden, down_proj, preferred_element_type=jnp.float32)
    added = lax.psum_scatter(down, "tp", scatter_dimension=0, tiled=True)
    share_slots = tp_index * share + jnp.arange(share, dtype=jnp.int32)
    live_share = (share_slots < length).astype(jnp.float32)
    layer_out = ((resid_share + added) * live_share[:, None]).astype(jnp.bfloat16)
    live_rows = (slots < length)[:, None]
    key_rows = keys16.reshape(seq_len, k_cols)
    value_rows = values16.reshape(seq_len, k_cols)
    cache_rows = jnp.concatenate(
        [
            jnp.where(live_rows, key_rows, jnp.zeros_like(key_rows)),
            jnp.where(live_rows, value_rows, jnp.zeros_like(value_rows)),
        ],
        axis=1,
    )
    pages = cache_rows.reshape(seq_len // PAGE, PAGE, 2 * k_cols)
    pool_size = pages.shape[0]
    owner = lax.axis_index("req")
    targets = owner * pool_size + jnp.arange(pool_size, dtype=jnp.int32)
    picks = (page_slot[:, None] == targets[None, :]).astype(jnp.bfloat16)
    pool = jnp.einsum(
        "np,nsc->psc",
        picks,
        lax.all_gather(pages, "req", axis=0, tiled=True),
        preferred_element_type=jnp.float32,
    )
    kv_cache = pool.astype(jnp.bfloat16)
    return (layer_out, kv_cache)


def solution(mesh):
    return jax.shard_map(
        body,
        mesh=mesh,
        in_specs=(
            P("req", None),
            P("req"),
            P(),
            P(),
            P(("req", "tp"), None),
            P(("req", "tp"), None),
            P(),
            P(),
            P("tp", None),
            P("tp", None),
        ),
        out_specs=(P(("req", "tp"), None), P("req", None, "tp")),
        check_vma=False,
    )
```

profile of v0, /device:TPU:1, one launch (start us, length us, event | category | flops | bytes accessed | tf_op | source)
XLA Modules:
  0.0 472.2 jit_solution(814724774709201183)
XLA Ops:
  7.2 1.2 convert_element_type.60
  8.4 0.9 all_to_all.28
  9.3 1.0 copy.18
  10.3 10.0 %all_to_all.38 = bf16[20,4,960]{2,0,1:T(8,128)(2,1)S(1)} all-to-all(bf16[20,4,960]{2,0,1:T(8,128)(2,1)S(1)} %copy.18), channel_id=1, replica_groups=mesh['req'=32,'tp'=4] {'tp'}, dimensions={1} | all-to-all | bytes 307200 | tf_op jit(solution)/shard_map/all_to_all | solution.py:58
  22.4 1.0 scatter_custom_fusion
  23.4 2.3 fusion.4
  26.1 0.8 fusion.26
  27.0 43.9 %all-gather.4.cloned.1.call-done = bf16[2560,960]{1,0:T(8,128)(2,1)} async-done(((bf16[80,960]{1,0:T(8,128)(2,1)}), bf16[2560,960]{1,0:T(8,128)(2,1)}) %all-gather.4.cloned.1.call-update) | async-done | bytes 4915216 | tf_op jit(solution)/shard_map/all_gather | solution.py:73
  70.9 9.7 %reshape.159 = bf16[128,20,960]{2,1,0:T(8,128)(2,1)} reshape(bf16[2560,960]{1,0:T(8,128)(2,1)} %all-gather.4.cloned.1.call-done) | data formatting | bytes 9830400 | tf_op jit(solution)/shard_map/reshape | solution.py:76
  80.6 6.4 %gather_fusion = bf16[128,20,960]{2,1,0:T(8,128)(2,1)} fusion(bf16[128,20,960]{2,1,0:T(8,128)(2,1)} %reshape.159, s32[1024]{0:T(1024)S(1)} %pad_clamp_fusion), kind=kCustom, calls=%fused_computation | custom fusion | bytes 9830912 | tf_op jit(solution)/shard_map/gather | solution.py:76
  87.0 9.8 %reshape.160 = bf16[2560,960]{1,0:T(8,128)(2,1)} reshape(bf16[128,20,960]{2,1,0:T(8,128)(2,1)} %gather_fusion) | data formatting | bytes 9830400 | tf_op jit(solution)/shard_map/reshape | solution.py:76
  96.8 6.2 %fusion.13 = f32[512,960]{0,1:T(8,128)S(1)} fusion(bf16[2560,960]{1,0:T(8,128)(2,1)} %reshape.160, bf16[512,2560]{1,0:T(8,128)(2,1)} %param.10, f32[2560]{0:T(1024)S(1)} %copy-done.7, f32[512]{0:T(512)S(1)} %add_rsqrt_fusion.1), kind=kOutput, calls=%fused_computation.25 | convolution fusion | flops 2521825280 | bytes 9515008 | tf_op jit(solution)/shard_map/dot_general | solution.py:82
  103.9 1.0 subtract_convert_fusion
  105.6 7.6 %fusion.49 = (f32[2,4,512]{2,1,0:T(4,128)S(1)}, f32[2,4,512,512]{2,3,1,0:T(8,128)}) fusion(pred[512,512]{0,1:T(8,128)(4,1)} %fusion.26, bf16[512,2,4,40]{0,3,2,1:T(8,128)(2,1)} %bitcast.65, bf16[512,2,4,40]{0,3,2,1:T(8,128)(2,1)} %bitcast.64, bf16[512,2,40]{0,2,1:T(8,128)(2,1)} %get-tuple-element.15, bf16[512,2,40]{0,2,1:T(8,128)(2,1)S(1)} %get-tuple-element.14), kind=kOutput, calls=%fused_computation.76 | convolution fusion | flops 345571840 | bytes 9486336 | tf_op jit(solution)/shard_map/sub | solution.py:99
  113.2 4.2 fusion.22
  117.4 4.6 fusion.54
  122.1 2.4 convert_element_type.68
  124.5 1.3 all_to_all.32
  125.9 21.6 %all_to_all.39 = bf16[20,4,3456]{2,0,1:T(8,128)(2,1)} all-to-all(bf16[20,4,3456]{2,0,1:T(8,128)(2,1)S(1)} %copy.20), channel_id=1, replica_groups=mesh['req'=32,'tp'=4] {'tp'}, dimensions={1} | all-to-all | bytes 1105920 | tf_op jit(solution)/shard_map/all_to_all | solution.py:61
  147.5 2.0 all_to_all.35
  150.8 86.5 %all-reduce.2.cloned.1.call-done = f32[512,2560]{1,0:T(8,128)} async-done(((f32[512,2560]{1,0:T(8,128)}), f32[512,2560]{1,0:T(8,128)}) %all-reduce.2.cloned.1.call-update) | async-done | bytes 5242896 | tf_op jit(solution)/shard_map/psum | solution.py:108
  237.4 5.4 %multiply_reduce_fusion = (f32[512]{0:T(512)S(1)}, f32[512,2560]{1,0:T(8,128)}) fusion(f32[512,2560]{1,0:T(8,128)} %all-reduce.2.cloned.1.call-done, bf16[512,2560]{1,0:T(8,128)(2,1)S(1)} %copy-done.2), kind=kLoop, calls=%fused_computation.17 | loop fusion | flops 5242368 | bytes 13109248 | tf_op jit(solution)/shard_map/reduce_sum | solution.py:13
  242.8 72.6 %all-gather.6.cloned.1.call-done = bf16[2560,3456]{1,0:T(8,128)(2,1)} async-done(((bf16[80,3456]{1,0:T(8,128)(2,1)}), bf16[2560,3456]{1,0:T(8,128)(2,1)}) %all-gather.6.cloned.1.call-update) | async-done | bytes 17694736 | tf_op jit(solution)/shard_map/all_gather | solution.py:74
  315.4 24.5 %reshape.164 = bf16[128,20,3456]{2,1,0:T(8,128)(2,1)} reshape(bf16[2560,3456]{1,0:T(8,128)(2,1)} %all-gather.6.cloned.1.call-done) | data formatting | bytes 35389440 | tf_op jit(solution)/shard_map/reshape | solution.py:79
  339.9 17.0 %gather_fusion.1 = bf16[128,20,3456]{2,1,0:T(8,128)(2,1)} fusion(bf16[128,20,3456]{2,1,0:T(8,128)(2,1)} %reshape.164, s32[1024]{0:T(1024)S(1)} %pad_clamp_fusion), kind=kCustom, calls=%fused_computation.1 | custom fusion | bytes 35389952 | tf_op jit(solution)/shard_map/gather | solution.py:79
  356.9 25.1 %reshape.165 = bf16[2560,3456]{1,0:T(8,128)(2,1)} reshape(bf16[128,20,3456]{2,1,0:T(8,128)(2,1)} %gather_fusion.1) | data formatting | bytes 35389440 | tf_op jit(solution)/shard_map/reshape | solution.py:79
  382.0 15.3 %fusion.12 = f32[512,3456]{1,0:T(8,128)S(1)} fusion(bf16[2560,3456]{1,0:T(8,128)(2,1)} %reshape.165, f32[512,2560]{1,0:T(8,128)} %get-tuple-element.11, f32[2560]{0:T(1024)S(1)} %copy-done.8, f32[512]{0:T(512)S(1)} %add_rsqrt_fusion), kind=kOutput, calls=%fused_computation.24 | convolution fusion | flops 9063628800 | bytes 30027776 | tf_op jit(solution)/shard_map/dot_general | solution.py:112
  397.3 10.4 %fusion.19 = f32[512,2560]{1,0:T(8,128)} fusion(bf16[1728,2560]{1,0:T(8,128)(2,1)} %param.19, f32[512,3456]{1,0:T(8,128)S(1)} %fusion.12), kind=kOutput, calls=%fused_computation.30 | convolution fusion | flops 4535156736 | bytes 21430272 | tf_op jit(solution)/shard_map/dot_general | solution.py:114
  408.4 9.9 %fusion.23 = bf16[4,128,320]{1,0,2:T(4,128)(2,1)S(1)} fusion(bf16[128,128,320]{1,2,0:T(8,128)(2,1)} %all-gather.8.cloned.1.call-done, s32[128]{0:T(128)S(1)} %copy-done.6, s32[4]{0:T(128)S(1)} %iota_add_fusion), kind=kOutput, calls=%fused_computation.34 | convolution fusion | flops 42107392 | bytes 10813968 | tf_op jit(solution)/shard_map/np,nsc->psc/dot_general | solution.py:134
  418.3 0.8 copy.24
  419.1 43.9 %reduce-scatter.2.cloned.1.call-done = f32[128,2560]{1,0:T(8,128)} async-done(((f32[512,2560]{1,0:T(8,128)}), f32[128,2560]{1,0:T(8,128)}) %reduce-scatter.2.cloned.1.call-update) | async-done | bytes 1310736 | tf_op jit(solution)/shard_map/reduce_scatter | solution.py:115
  462.9 2.7 multiply_convert_fusion.2
  (52 shorter events, 5.4 us)
Async XLA Ops:
  7.2 110.3 %copy-start = (bf16[640,2560]{1,0:T(8,128)(2,1)S(1)}, bf16[640,2560]{1,0:T(8,128)(2,1)}, u32[]{:S(2)}) copy-start(bf16[640,2560]{1,0:T(8,128)(2,1)} %param.18) | copy-start | bytes 9830404
  7.2 63.7 %all-gather.4.cloned.1.call-start = ((), (), s32[]{:S(2)}) async-start(), calls=%async_computation.3 | async-start | bytes 5406720 | tf_op jit(solution)/shard_map/all_gather | solution.py:73
  21.0 216.3 %all-reduce.2.cloned.1.call-start = ((), (), s32[]{:S(2)}) async-start(), calls=%async_computation.4 | async-start | bytes 10485760 | tf_op jit(solution)/shard_map/psum | solution.py:108
  87.0 9.8 %copy-start.7 = (f32[2560]{0:T(1024)S(1)}, f32[2560]{0:T(1024)}, u32[]{:S(2)}) copy-start(f32[2560]{0:T(1024)} %param.16) | copy-start | bytes 30724
  105.6 7.6 %copy-start.5 = (bf16[512,160]{0,1:T(8,128)(2,1)S(1)}, bf16[512,160]{0,1:T(8,128)(2,1)}, u32[]{:S(2)}) copy-start(bf16[512,160]{0,1:T(8,128)(2,1)} %get-tuple-element.9) | copy-start | bytes 491524
  122.0 27.8 %copy-start.3 = (bf16[20,4,8,128]{3,2,1,0:T(8,128)(2,1)S(1)}, bf16[20,4,8,128]{3,2,1,0:T(8,128)(2,1)}, u32[]{:S(2)}) copy-start(bf16[20,4,8,128]{3,2,1,0:T(8,128)(2,1)} %get-tuple-element.8) | copy-start | bytes 491524
  122.0 27.8 %copy-start.4 = (bf16[512,2,40]{0,2,1:T(8,128)(2,1)S(1)}, bf16[512,2,40]{0,2,1:T(8,128)(2,1)}, u32[]{:S(2)}) copy-start(bf16[512,2,40]{0,2,1:T(8,128)(2,1)} %get-tuple-element.15) | copy-start | bytes 245764
  122.0 115.3 %copy-start.2 = (bf16[512,2560]{1,0:T(8,128)(2,1)S(1)}, bf16[512,2560]{1,0:T(8,128)(2,1)}, u32[]{:S(2)}) copy-start(bf16[512,2560]{1,0:T(8,128)(2,1)} %param.10) | copy-start | bytes 7864324
  122.1 193.3 %all-gather.6.cloned.1.call-start = ((), (), s32[]{:S(2)}) async-start(), calls=%async_computation.5 | async-start | bytes 18247680 | tf_op jit(solution)/shard_map/all_gather | solution.py:74
  149.6 258.2 %all-gather.8.cloned.1.call-start = ((), (), s32[]{:S(2)}) async-start(), calls=%async_computation.7 | async-start | bytes 10813440 | tf_op jit(solution)/shard_map/all_gather | solution.py:137
  150.8 312.2 %reduce-scatter.2.cloned.1.call-start = ((), (), s32[]{:S(2)}) async-start(), calls=%async_computation.6 | async-start | bytes 6553600 | tf_op jit(solution)/shard_map/reduce_scatter | solution.py:115
  356.9 25.1 %copy-start.8 = (f32[2560]{0:T(1024)S(1)}, f32[2560]{0:T(1024)}, u32[]{:S(2)}) copy-start(f32[2560]{0:T(1024)} %param.17) | copy-start | bytes 30724
  407.7 0.7 copy-start.6
  407.8 57.9 %copy-start.1 = (bf16[640,2560]{1,0:T(8,128)(2,1)S(1)}, bf16[640,2560]{1,0:T(8,128)(2,1)}, u32[]{:S(2)}) copy-start(bf16[640,2560]{1,0:T(8,128)(2,1)} %param.18) | copy-start | bytes 9830404
Sparse Core Ops, SparseCore 0:
  21.1 49.7 all-gather.3
  122.2 115.1 all-reduce.1
  240.3 75.0 all-gather.5
  318.1 57.3 all-gather.7
  407.9 55.0 reduce-scatter.1
where the time goes:
time: 474 us; the launch traced here: 472 us
  waiting for transfers between devices  247 us (52%)
  local copies, waits for them, and re-layouts  101 us (21%)
  matrix products  58.2 us (12%)
  blocking collectives  31.6 us (7%)
  other arithmetic  19.2 us (4%)
  between operations  14.6 us (3%)
    psum x1, waiting for transfers between devices, body(): mixed = lax.psum(partial_out, 'tp')  86.5 us
    all_gather x1, waiting for transfers between devices, body(): lax.all_gather(gu_half, 'req', axis=0, tiled=True)  72.6 us
    reshape x2, local copies, waits for them, and re-layouts, body(): gu_all.reshape(devices, rows_each, gu_all.shape[1])[inverse]  49.7 us
    all_gather x1, waiting for transfers between devices, body(): lax.all_gather(qkv_half, 'req', axis=0, tiled=True)  43.9 us
    reduce_scatter x1, waiting for transfers between devices, body(): added = lax.psum_scatter(down, 'tp', scatter_dimension=0, tiled=True)  43.9 us
    all_to_all x1, blocking collectives, body(): lax.all_to_all(trainer_gateup.astype(jnp.bfloat16), 'tp', split_axis=1, c...  21.6 us
    reshape x2, local copies, waits for them, and re-layouts, body(): qkv_all.reshape(devices, rows_each, qkv_all.shape[1])[inverse]  19.5 us
    gather x1, local copies, waits for them, and re-layouts, body(): gu_all.reshape(devices, rows_each, gu_all.shape[1])[inverse]  17 us
  transfers between devices with their start and end apart: 5, of which 4 were waited for; matrix products, arithmetic and copies ran while one was open for 25% of the time, Pallas kernels for 0%

commit v1 on v0

--- a/solution.py
+++ b/solution.py
@@ -1,3 +1,4 @@
+import functools
 import jax
 import jax.numpy as jnp
 from jax import lax
@@ -7,6 +8,38 @@
 PAGE = 128
 eps_norm = 1e-05
 theta_base = 10000.0
+
+
+def form_the_patches(message, along_dim, matrix):
+    n_now = message.shape
+    part_now = message.reshape(
+        *n_now[:along_dim], matrix, n_now[along_dim] // matrix, *n_now[along_dim + 1 :]
+    )
+    return jnp.moveaxis(part_now, along_dim, 0)
+
+
+def advance_chunk_on_mesh(shard_in, dim_no):
+    inter = list(shard_in.shape[1:])
+    inter[dim_no] *= shard_in.shape[0]
+    return jnp.moveaxis(shard_in, 0, dim_no).reshape(inter)
+
+
+def produce_the_stops_all(block_here, which_axis, inp, patch):
+    arr_next = lax.axis_index(which_axis)
+    high = lax.axis_size(which_axis)
+    u_next, reply = (high, arr_next)
+    left_arr = form_the_patches(block_here, inp, u_next)
+    entries = [left_arr[reply]]
+    for j0 in range(1, u_next):
+        seen_now = left_arr[reply ^ j0]
+        mat_out = lax.ppermute(seen_now, which_axis, [(d, d ^ j0) for d in range(u_next)])
+        entries.append(mat_out)
+    s_next = jnp.stack(entries)
+    left_arr = s_next[reply ^ jnp.arange(u_next)]
+    return advance_chunk_on_mesh(left_arr, patch)
+
+
+derive_the_sections = functools.partial(produce_the_stops_all, which_axis="tp", inp=1, patch=0)
 
 
 def normed(values, gain):
@@ -55,9 +88,7 @@
     k_cols = local_kv * head_dim
     ff_local = down_proj.shape[0]
     qkv_half, gu_half = (
-        lax.all_to_all(
-            trainer_qkv.astype(jnp.bfloat16), "tp", split_axis=1, concat_axis=0, tiled=True
-        ),
+        derive_the_sections(trainer_qkv.astype(jnp.bfloat16)),
         lax.all_to_all(
             trainer_gateup.astype(jnp.bfloat16), "tp", split_axis=1, concat_axis=0, tiled=True
         ),

time: 474 us -> 476 us (level)
  blocking collectives: 31.6 us -> 21.6 us
  waiting for transfers between devices: 247 us -> 252 us
    all_to_all x1 -> x0, blocking collectives: 9.99 us -> none  [body(): lax.all_to_all(trainer_qkv.astype(jnp.bfloat16), 'tp', split_axis=1, conc...]
  transfers between devices with their start and end apart: 5 -> 8, of which waited for: 4 -> 6; matrix products, arithmetic and copies ran while one was open for 25% -> 25% of each run, Pallas kernels for 0% -> 0%
where the time goes in v1:
time: 476 us; the launch traced here: 474 us
  waiting for transfers between devices  252 us (53%)
  local copies, waits for them, and re-layouts  103 us (22%)
  matrix products  58.2 us (12%)
  blocking collectives  21.6 us (5%)
  other arithmetic  19.9 us (4%)
  between operations  14.7 us (3%)
  starting transfers between devices  4.82 us (1%)
    psum x1, waiting for transfers between devices, body(): mixed = lax.psum(partial_out, 'tp')  86.5 us
    all_gather x1, waiting for transfers between devices, body(): lax.all_gather(gu_half, 'req', axis=0, tiled=True)  72.6 us
    reshape x2, local copies, waits for them, and re-layouts, body(): gu_all.reshape(devices, rows_each, gu_all.shape[1])[inverse]  49.7 us
    all_gather x1, waiting for transfers between devices, body(): lax.all_gather(qkv_half, 'req', axis=0, tiled=True)  44.7 us
    reduce_scatter x1, waiting for transfers between devices, body(): added = lax.psum_scatter(down, 'tp', scatter_dimension=0, tiled=True)  43.9 us
    all_to_all x1, blocking collectives, body(): lax.all_to_all(trainer_gateup.astype(jnp.bfloat16), 'tp', split_axis=1, c...  21.6 us
    reshape x2, local copies, waits for them, and re-layouts, body(): qkv_all.reshape(devices, rows_each, qkv_all.shape[1])[inverse]  19.5 us
    gather x1, local copies, waits for them, and re-layouts, body(): gu_all.reshape(devices, rows_each, gu_all.shape[1])[inverse]  17 us
  transfers between devices with their start and end apart: 8, of which 6 were waited for; matrix products, arithmetic and copies ran while one was open for 25% of the time, Pallas kernels for 0%

profile of v1, /device:TPU:1, one launch (start us, length us, event | category | flops | bytes accessed | tf_op | source)
XLA Modules:
  0.0 474.0 jit_solution(2891430676380902186)
XLA Ops:
  7.2 1.8 convert_element_type.60
  9.1 1.2 reshape.185
  10.6 3.6 collective-permute-start.2
  15.8 3.1 collective-permute-done.1
  18.9 1.2 gather_fusion
  20.1 1.6 reshape.186
  23.1 1.2 scatter_custom_fusion
  24.4 2.3 fusion.4
  27.9 44.7 %all-gather.4.cloned.1.call-done = bf16[2560,960]{1,0:T(8,128)(2,1)} async-done(((bf16[80,960]{1,0:T(8,128)(2,1)}), bf16[2560,960]{1,0:T(8,128)(2,1)}) %all-gather.4.cloned.1.call-update) | async-done | bytes 4915216 | tf_op jit(solution)/shard_map/all_gather | solution.py:104
  72.6 9.7 %reshape.187 = bf16[128,20,960]{2,1,0:T(8,128)(2,1)} reshape(bf16[2560,960]{1,0:T(8,128)(2,1)} %all-gather.4.cloned.1.call-done) | data formatting | bytes 9830400 | tf_op jit(solution)/shard_map/reshape | solution.py:107
  82.4 6.4 %gather_fusion.1 = bf16[128,20,960]{2,1,0:T(8,128)(2,1)} fusion(bf16[128,20,960]{2,1,0:T(8,128)(2,1)} %reshape.187, s32[1024]{0:T(1024)S(1)} %pad_clamp_fusion), kind=kCustom, calls=%fused_computation.1 | custom fusion | bytes 9830912 | tf_op jit(solution)/shard_map/gather | solution.py:107
  88.7 9.8 %reshape.188 = bf16[2560,960]{1,0:T(8,128)(2,1)} reshape(bf16[128,20,960]{2,1,0:T(8,128)(2,1)} %gather_fusion.1) | data formatting | bytes 9830400 | tf_op jit(solution)/shard_map/reshape | solution.py:107
  98.5 6.2 %fusion.13 = f32[512,960]{0,1:T(8,128)S(1)} fusion(bf16[2560,960]{1,0:T(8,128)(2,1)} %reshape.188, bf16[512,2560]{1,0:T(8,128)(2,1)} %param.10, f32[2560]{0:T(1024)S(1)} %copy-done.7, f32[512]{0:T(512)S(1)} %add_rsqrt_fusion.1), kind=kOutput, calls=%fused_computation.26 | convolution fusion | flops 2521825280 | bytes 9515008 | tf_op jit(solution)/shard_map/dot_general | solution.py:113
  105.6 1.0 subtract_convert_fusion
  107.3 7.6 %fusion.50 = (f32[2,4,512]{2,1,0:T(4,128)S(1)}, f32[2,4,512,512]{2,3,1,0:T(8,128)}) fusion(pred[512,512]{0,1:T(8,128)(4,1)} %fusion.26, bf16[512,2,4,40]{0,3,2,1:T(8,128)(2,1)} %bitcast.80, bf16[512,2,4,40]{0,3,2,1:T(8,128)(2,1)} %bitcast.79, bf16[512,2,40]{0,2,1:T(8,128)(2,1)} %get-tuple-element.17, bf16[512,2,40]{0,2,1:T(8,128)(2,1)S(1)} %get-tuple-element.16), kind=kOutput, calls=%fused_computation.89 | convolution fusion | flops 345571840 | bytes 9486336 | tf_op jit(solution)/shard_map/sub | solution.py:130
  114.9 4.2 fusion.22
  119.1 4.6 fusion.55
  123.8 2.4 convert_element_type.68
  126.2 1.3 all_to_all.14
  127.6 21.6 %all_to_all.19 = bf16[20,4,3456]{2,0,1:T(8,128)(2,1)} all-to-all(bf16[20,4,3456]{2,0,1:T(8,128)(2,1)S(1)} %copy.21), channel_id=1, replica_groups=mesh['req'=32,'tp'=4] {'tp'}, dimensions={1} | all-to-all | bytes 1105920 | tf_op jit(solution)/shard_map/all_to_all | solution.py:92
  149.2 2.0 all_to_all.17
  152.5 86.5 %all-reduce.2.cloned.1.call-done = f32[512,2560]{1,0:T(8,128)} async-done(((f32[512,2560]{1,0:T(8,128)}), f32[512,2560]{1,0:T(8,128)}) %all-reduce.2.cloned.1.call-update) | async-done | bytes 5242896 | tf_op jit(solution)/shard_map/psum | solution.py:139
  239.1 5.4 %multiply_reduce_fusion = (f32[512]{0:T(512)S(1)}, f32[512,2560]{1,0:T(8,128)}) fusion(f32[512,2560]{1,0:T(8,128)} %all-reduce.2.cloned.1.call-done, bf16[512,2560]{1,0:T(8,128)(2,1)S(1)} %copy-done.2), kind=kLoop, calls=%fused_computation.18 | loop fusion | flops 5242368 | bytes 13109248 | tf_op jit(solution)/shard_map/reduce_sum | solution.py:46
  244.5 72.6 %all-gather.6.cloned.1.call-done = bf16[2560,3456]{1,0:T(8,128)(2,1)} async-done(((bf16[80,3456]{1,0:T(8,128)(2,1)}), bf16[2560,3456]{1,0:T(8,128)(2,1)}) %all-gather.6.cloned.1.call-update) | async-done | bytes 17694736 | tf_op jit(solution)/shard_map/all_gather | solution.py:105
  317.1 24.6 %reshape.192 = bf16[128,20,3456]{2,1,0:T(8,128)(2,1)} reshape(bf16[2560,3456]{1,0:T(8,128)(2,1)} %all-gather.6.cloned.1.call-done) | data formatting | bytes 35389440 | tf_op jit(solution)/shard_map/reshape | solution.py:110
  341.7 17.0 %gather_fusion.2 = bf16[128,20,3456]{2,1,0:T(8,128)(2,1)} fusion(bf16[128,20,3456]{2,1,0:T(8,128)(2,1)} %reshape.192, s32[1024]{0:T(1024)S(1)} %pad_clamp_fusion), kind=kCustom, calls=%fused_computation.2 | custom fusion | bytes 35389952 | tf_op jit(solution)/shard_map/gather | solution.py:110
  358.6 25.1 %reshape.193 = bf16[2560,3456]{1,0:T(8,128)(2,1)} reshape(bf16[128,20,3456]{2,1,0:T(8,128)(2,1)} %gather_fusion.2) | data formatting | bytes 35389440 | tf_op jit(solution)/shard_map/reshape | solution.py:110
  383.8 15.3 %fusion.12 = f32[512,3456]{1,0:T(8,128)S(1)} fusion(bf16[2560,3456]{1,0:T(8,128)(2,1)} %reshape.193, f32[512,2560]{1,0:T(8,128)} %get-tuple-element.13, f32[2560]{0:T(1024)S(1)} %copy-done.8, f32[512]{0:T(512)S(1)} %add_rsqrt_fusion), kind=kOutput, calls=%fused_computation.25 | convolution fusion | flops 9063628800 | bytes 30027776 | tf_op jit(solution)/shard_map/dot_general | solution.py:143
  399.1 10.4 %fusion.19 = f32[512,2560]{1,0:T(8,128)} fusion(bf16[1728,2560]{1,0:T(8,128)(2,1)} %param.19, f32[512,3456]{1,0:T(8,128)S(1)} %fusion.12), kind=kOutput, calls=%fused_computation.31 | convolution fusion | flops 4535156736 | bytes 21430272 | tf_op jit(solution)/shard_map/dot_general | solution.py:145
  410.2 9.9 %fusion.23 = bf16[4,128,320]{1,0,2:T(4,128)(2,1)S(1)} fusion(bf16[128,128,320]{1,2,0:T(8,128)(2,1)} %all-gather.8.cloned.1.call-done, s32[128]{0:T(128)S(1)} %copy-done.6, s32[4]{0:T(128)S(1)} %iota_add_fusion), kind=kOutput, calls=%fused_computation.35 | convolution fusion | flops 42107392 | bytes 10813968 | tf_op jit(solution)/shard_map/np,nsc->psc/dot_general | solution.py:165
  420.9 43.9 %reduce-scatter.2.cloned.1.call-done = f32[128,2560]{1,0:T(8,128)} async-done(((f32[512,2560]{1,0:T(8,128)}), f32[128,2560]{1,0:T(8,128)}) %reduce-scatter.2.cloned.1.call-update) | async-done | bytes 1310736 | tf_op jit(solution)/shard_map/reduce_scatter | solution.py:146
  464.8 2.7 multiply_convert_fusion.2
  (65 shorter events, 8.2 us)
Async XLA Ops:
  7.2 112.0 %copy-start = (bf16[640,2560]{1,0:T(8,128)(2,1)S(1)}, bf16[640,2560]{1,0:T(8,128)(2,1)}, u32[]{:S(2)}) copy-start(bf16[640,2560]{1,0:T(8,128)(2,1)} %param.18) | copy-start | bytes 9830404
  7.2 65.4 %all-gather.4.cloned.1.call-start = ((), (), s32[]{:S(2)}) async-start(), calls=%async_computation.2 | async-start | bytes 5406720 | tf_op jit(solution)/shard_map/all_gather | solution.py:104
  10.6 5.1 %collective-permute-start.2 = (bf16[20,960]{1,0:T(8,128)(2,1)S(1)}, bf16[20,960]{1,0:T(8,128)(2,1)S(1)}, u32[]{:S(2)}, u32[]{:S(2)}) collective-permute-start(bf16[20,960]{1,0:T(8,128)(2,1)S(1)} %bitcast.86), channel_id=1, source_target_pairs={{0,3},{1,2},{2,1},{3,0},{4,7},{5,6},{6,5},{7,4},{8,11},{9,10},{10,... | collective-permute-start | bytes 115208 | tf_op jit(solution)/shard_map/ppermute | solution.py:35
  14.3 4.5 collective-permute-start.1
  14.8 4.1 collective-permute-start
  21.8 217.3 %all-reduce.2.cloned.1.call-start = ((), (), s32[]{:S(2)}) async-start(), calls=%async_computation.3 | async-start | bytes 10485760 | tf_op jit(solution)/shard_map/psum | solution.py:139
  88.7 9.8 %copy-start.7 = (f32[2560]{0:T(1024)S(1)}, f32[2560]{0:T(1024)}, u32[]{:S(2)}) copy-start(f32[2560]{0:T(1024)} %param.16) | copy-start | bytes 30724
  107.3 7.6 %copy-start.5 = (bf16[512,160]{0,1:T(8,128)(2,1)S(1)}, bf16[512,160]{0,1:T(8,128)(2,1)}, u32[]{:S(2)}) copy-start(bf16[512,160]{0,1:T(8,128)(2,1)} %get-tuple-element.11) | copy-start | bytes 491524
  123.7 27.8 %copy-start.3 = (bf16[20,4,8,128]{3,2,1,0:T(8,128)(2,1)S(1)}, bf16[20,4,8,128]{3,2,1,0:T(8,128)(2,1)}, u32[]{:S(2)}) copy-start(bf16[20,4,8,128]{3,2,1,0:T(8,128)(2,1)} %get-tuple-element.10) | copy-start | bytes 491524
  123.7 27.9 %copy-start.4 = (bf16[512,2,40]{0,2,1:T(8,128)(2,1)S(1)}, bf16[512,2,40]{0,2,1:T(8,128)(2,1)}, u32[]{:S(2)}) copy-start(bf16[512,2,40]{0,2,1:T(8,128)(2,1)} %get-tuple-element.17) | copy-start | bytes 245764
  123.7 115.3 %copy-start.2 = (bf16[512,2560]{1,0:T(8,128)(2,1)S(1)}, bf16[512,2560]{1,0:T(8,128)(2,1)}, u32[]{:S(2)}) copy-start(bf16[512,2560]{1,0:T(8,128)(2,1)} %param.10) | copy-start | bytes 7864324
  123.8 193.3 %all-gather.6.cloned.1.call-start = ((), (), s32[]{:S(2)}) async-start(), calls=%async_computation.4 | async-start | bytes 18247680 | tf_op jit(solution)/shard_map/all_gather | solution.py:105
  151.3 258.4 %all-gather.8.cloned.1.call-start = ((), (), s32[]{:S(2)}) async-start(), calls=%async_computation.6 | async-start | bytes 10813440 | tf_op jit(solution)/shard_map/all_gather | solution.py:168
  152.5 312.3 %reduce-scatter.2.cloned.1.call-start = ((), (), s32[]{:S(2)}) async-start(), calls=%async_computation.5 | async-start | bytes 6553600 | tf_op jit(solution)/shard_map/reduce_scatter | solution.py:146
  358.6 25.1 %copy-start.8 = (f32[2560]{0:T(1024)S(1)}, f32[2560]{0:T(1024)}, u32[]{:S(2)}) copy-start(f32[2560]{0:T(1024)} %param.17) | copy-start | bytes 30724
  409.6 0.7 copy-start.6
  409.6 57.9 %copy-start.1 = (bf16[640,2560]{1,0:T(8,128)(2,1)S(1)}, bf16[640,2560]{1,0:T(8,128)(2,1)}, u32[]{:S(2)}) copy-start(bf16[640,2560]{1,0:T(8,128)(2,1)} %param.18) | copy-start | bytes 9830404
Sparse Core Ops, SparseCore 0:
  21.9 50.6 all-gather.3
  123.9 115.1 all-reduce.1
  242.0 75.0 all-gather.5
  319.8 57.3 all-gather.7
  409.7 55.0 reduce-scatter.1
